TPU v7x, 32 devices: a whole 2x2x4 slice. The times are simulated.
32 devices in a mesh: blk: 4 (over y, x), dp: 8 (over z, core).
Axes of the slice: x: 2, y: 2, z: 4, core: 2. Of those that a mesh axis runs over, the one named last changes fastest.
Arguments:
- patches: bfloat16 [4096, 64, 256], P(('blk', 'dp')), may hold values from -6 to 6
- w_mix: bfloat16 [256, 128], replicated, may hold values from -0.375 to 0.375
- w_in: bfloat16 [2048, 512], replicated, may hold values from -0.125 to 0.125
- w_out: bfloat16 [512, 128], replicated, may hold values from -0.25 to 0.25
- partner_dev: int32 [4096], P(('blk', 'dp')), may hold values from 0 to 7, as said below
- partner_row: int32 [4096], P(('blk', 'dp')), may hold values from 0 to 127, as said below
Outputs:
- loss_rows: float32 [4096], P(('blk', 'dp'))
- grad_mix: float32 [256, 128], replicated
- grad_in: float32 [2048, 512], replicated
- grad_out: float32 [512, 128], replicated
Inputs may be any that keep to these rules, and one draw needn't show every extreme that they name: Among one device's rows every dp index appears as partner_dev exactly 128/8 times. Over the rows that share a blk index, the pairs (partner_dev, partner_row) name every pair of dp index and row of a device exactly once.
All inputs are finite; a program needn't handle non-finite values.
Results may differ from a plain program's by a relative error of at most 0.012.
The roundings to bfloat16 on the way count: a program that leaves them out, or rounds other values in their place, can miss the bound.
Values may be sent and summed in bfloat16 or wider, within the bound.
No kernel may reach another device: no remote copies, remote signals or barrier semaphores. Data moves between devices by JAX's collectives and lax.ppermute only.
A program may use at most 64 MiB of HBM per device.

v0:
```python
import math
import jax
import jax.numpy as jnp
from jax import lax
from jax.sharding import PartitionSpec as P

SCALE = 10.0


def dft_table(length, freqs):
    angle_idx = jnp.arange(length, dtype=jnp.int32)
    freq_idx = jnp.arange(freqs, dtype=jnp.int32)
    phase = jnp.mod(freq_idx[None, :] * angle_idx[:, None], length).astype(jnp.float32) * (
        2.0 * math.pi / length
    )
    return jnp.concatenate([jnp.cos(phase), -jnp.sin(phase)], axis=1).astype(jnp.bfloat16)


def encode(block, w_mix, w_in, w_out):
    count, length, lanes = block.shape
    filters = w_mix.shape[1]
    freqs = w_in.shape[0] // filters
    angle_table = dft_table(length, freqs)
    spec = jnp.einsum("pac,ak->pkc", block, angle_table, preferred_element_type=jnp.float32).astype(
        jnp.bfloat16
    )
    mixed = jnp.dot(spec.reshape(-1, lanes), w_mix, preferred_element_type=jnp.float32).reshape(
        count, 2 * freqs, filters
    )
    real_part = mixed[:, :freqs]
    imag_part = mixed[:, freqs:]
    powers = real_part * real_part + imag_part * imag_part
    features = jnp.log1p(powers).reshape(count, -1)
    mean_removed = features - jnp.mean(features, axis=1, keepdims=True)
    reciprocal_scale = lax.rsqrt(
        jnp.mean(mean_removed * mean_removed, axis=1, keepdims=True) + 1e-05
    )
    normed = (mean_removed * reciprocal_scale).astype(jnp.bfloat16)
    preact = jnp.dot(normed, w_in, preferred_element_type=jnp.float32)
    hidden = jax.nn.silu(preact).astype(jnp.bfloat16)
    raw_embed = jnp.dot(hidden, w_out, preferred_element_type=jnp.float32)
    norms = jnp.sqrt(jnp.sum(raw_embed * raw_embed, axis=1, keepdims=True) + 1e-06)
    unit32 = raw_embed / norms
    saved = (
        spec,
        real_part,
        imag_part,
        powers,
        mean_removed,
        reciprocal_scale,
        normed,
        preact,
        hidden,
        unit32,
        norms,
    )
    return (unit32.astype(jnp.bfloat16), saved)


def back_upper(grad_units, saved, w_in, w_out):
    (
        spec,
        real_part,
        imag_part,
        powers,
        mean_removed,
        reciprocal_scale,
        normed,
        preact,
        hidden,
        unit32,
        norms,
    ) = saved
    grad_raw = (
        (grad_units - unit32 * jnp.sum(unit32 * grad_units, axis=1, keepdims=True)) / norms
    ).astype(jnp.bfloat16)
    g_out = jnp.dot(hidden.T, grad_raw, preferred_element_type=jnp.float32)
    grad_hid = jnp.dot(grad_raw, w_out.T, preferred_element_type=jnp.float32)
    sigm = jax.nn.sigmoid(preact)
    grad_pre = (grad_hid * sigm * (1.0 + preact * (1.0 - sigm))).astype(jnp.bfloat16)
    g_in = jnp.dot(normed.T, grad_pre, preferred_element_type=jnp.float32)
    norm_gradient = jnp.dot(grad_pre, w_in.T, preferred_element_type=jnp.float32)
    return (g_in, g_out, norm_gradient)


def back_lower(norm_gradient, saved):
    (
        spec,
        real_part,
        imag_part,
        powers,
        mean_removed,
        reciprocal_scale,
        normed,
        preact,
        hidden,
        unit32,
        norms,
    ) = saved
    lanes = spec.shape[2]
    normalized_input = mean_removed * reciprocal_scale
    feature_gradient = reciprocal_scale * (
        norm_gradient
        - jnp.mean(norm_gradient, axis=1, keepdims=True)
        - normalized_input * jnp.mean(norm_gradient * normalized_input, axis=1, keepdims=True)
    )
    grad_pow = feature_gradient.reshape(powers.shape) / (1.0 + powers)
    grad_mixed = jnp.concatenate(
        [2.0 * real_part * grad_pow, 2.0 * imag_part * grad_pow], axis=1
    ).astype(jnp.bfloat16)
    return jnp.dot(
        spec.reshape(-1, lanes).T,
        grad_mixed.reshape(-1, grad_mixed.shape[2]),
        preferred_element_type=jnp.float32,
    )


def negative_part(units, piece, row_ids):
    scores = SCALE * jnp.dot(units, piece.T, preferred_element_type=jnp.float32)
    column = jnp.arange(piece.shape[0], dtype=jnp.int32)
    expo = jnp.where(column[None, :] == row_ids[:, None], jnp.float32(0.0), jnp.exp(scores))
    return (
        jnp.sum(expo, axis=1),
        jnp.dot(expo.astype(jnp.bfloat16), piece, preferred_element_type=jnp.float32),
    )


def key_part(units, piece, tot_piece, row_ids):
    scores = SCALE * jnp.dot(piece, units.T, preferred_element_type=jnp.float32)
    column = jnp.arange(piece.shape[0], dtype=jnp.int32)
    expo = jnp.where(column[:, None] == row_ids[None, :], jnp.float32(0.0), jnp.exp(scores))
    weights = (expo / tot_piece[:, None]).astype(jnp.bfloat16)
    return jnp.dot(weights.T, piece, preferred_element_type=jnp.float32)


def on_device(patches, w_mix, w_in, w_out, partner_dev, partner_row):
    count = patches.shape[0]
    embed = w_out.shape[1]
    units, saved = encode(patches, w_mix, w_in, w_out)
    peers = lax.axis_size("dp")
    per_peer = count // peers
    sorted_positions = jnp.argsort(partner_dev, stable=True)
    inverse = jnp.argsort(sorted_positions, stable=True)
    wanted = partner_row[sorted_positions].reshape(peers, per_peer)
    asked = lax.all_to_all(wanted, "dp", split_axis=0, concat_axis=0, tiled=True)
    picked = units[asked]
    returned_rows = lax.all_to_all(picked, "dp", split_axis=0, concat_axis=0, tiled=True)
    positive = returned_rows.reshape(count, embed)[inverse]
    spos = SCALE * jnp.sum(units.astype(jnp.float32) * positive.astype(jnp.float32), axis=1)
    row_ids = lax.axis_index("blk") * count + jnp.arange(count, dtype=jnp.int32)
    zpart, npart = negative_part(units, lax.all_gather(units, "blk", axis=0, tiled=True), row_ids)
    totals = jnp.exp(spos) + zpart
    all_totals = lax.all_gather(totals, "blk", axis=0, tiled=True)
    keyterm = key_part(units, lax.all_gather(units, "blk", axis=0, tiled=True), all_totals, row_ids)
    loss_rows = jnp.log(totals) - spos
    coef = SCALE / count
    ppos = jnp.exp(spos) / totals
    partner_grad = coef * (ppos - 1.0)[:, None] * units.astype(jnp.float32)
    outgoing = partner_grad[sorted_positions].reshape(peers, per_peer, embed)
    incoming = lax.all_to_all(outgoing, "dp", split_axis=0, concat_axis=0, tiled=True)
    from_partner = (
        jnp.zeros((count, embed), jnp.float32)
        .at[asked.reshape(-1)]
        .add(incoming.reshape(-1, embed))
    )
    grad_units = (
        coef * ((ppos - 1.0)[:, None] * positive.astype(jnp.float32) + npart / totals[:, None])
        + coef * keyterm
        + from_partner
    )
    g_in, g_out, norm_gradient = back_upper(grad_units, saved, w_in, w_out)
    g_mix = back_lower(norm_gradient, saved)
    g_mix, g_in, g_out = lax.psum((g_mix, g_in, g_out), ("blk", "dp"))
    return (loss_rows, g_mix, g_in, g_out)


def solution(mesh):
    placed = (P(("blk", "dp"), None, None), P(), P(), P(), P(("blk", "dp")), P(("blk", "dp")))
    return jax.shard_map(
        on_device,
        mesh=mesh,
        in_specs=placed,
        out_specs=(P(("blk", "dp")), P(), P(), P()),
        check_vma=False,
    )
```

profile of v0, /device:TPU:0, one launch (start us, length us, event | category | flops | bytes accessed | tf_op | source)
XLA Modules:
  0.0 252.2 jit_solution(4154058484988354202)
XLA Ops:
  7.2 3.3 %sort.31 = (s32[128]{0:T(128)}, s32[128]{0:T(128)S(1)}) sort(s32[128]{0:T(128)} %param.10, s32[128]{0:T(128)S(1)} %iota.30), dimensions={0}, to_apply=%region_3.4 | sort | flops 896 | bytes 2048 | tf_op jit(solution)/shard_map/jit(argsort)/sort | solution.py:142
  10.5 1.6 gather_fusion
  12.8 6.4 %all-to-all-start = ((s32[8,1,16]{2,1,0:T(1,128)}), s32[8,1,16]{2,1,0:T(1,128)S(1)}, u32[]{:S(2)}, u32[]{:S(2)}) async-start(s32[8,1,16]{2,1,0:T(1,128)} %bitcast.4), calls=%async_computation | async-start | bytes 8192 | tf_op jit(solution)/shard_map/all_to_all | solution.py:145
  19.3 2.5 %sort.32 = (s32[128]{0:T(128)}, s32[128]{0:T(128)S(1)}) sort(s32[128]{0:T(128)S(1)} %get-tuple-element.6, s32[128]{0:T(128)S(1)} %iota.31), dimensions={0}, to_apply=%region_4.5 | sort | flops 896 | bytes 2048 | tf_op jit(solution)/shard_map/jit(argsort)/sort | solution.py:143
  21.8 2.9 %convert_bitcast_fusion = bf16[128,32,256]{2,1,0:T(8,128)(2,1)S(1)} fusion(bf16[128,64,256]{2,1,0:T(8,128)(2,1)} %param.6, bf16[64,16]{0,1:T(8,128)(2,1)S(1)} %get-tuple-element.27, bf16[64,16]{0,1:T(8,128)(2,1)S(1)} %get-tuple-element.28), kind=kOutput, calls=%fused_computation.7 | convolution fusion | flops 135274496 | bytes 6295552 | tf_op jit(solution)/shard_map/pac,ak->pkc/dot_general | solution.py:24
  24.8 2.5 fusion
  28.9 1.6 copy.38
  30.5 1.2 multiply_convert_fusion.2
  32.0 8.5 %all_gather.7 = bf16[512,128]{0,1:T(8,128)(2,1)S(1)} all-gather(bf16[128,128]{0,1:T(8,128)(2,1)S(1)} %fusion.35), channel_id=1, replica_groups=mesh['blk'=4,'dp'=8] {'blk'}, dimensions={0}, use_global_device_ids=true | all-gather | bytes 163840 | tf_op jit(solution)/shard_map/all_gather | solution.py:151
  42.9 1.3 gather_fusion.1
  44.2 5.1 %all-to-all-start.1 = ((bf16[8,16,128]{2,1,0:T(8,128)(2,1)}), bf16[8,16,128]{2,1,0:T(8,128)(2,1)S(1)}, u32[]{:S(2)}, u32[]{:S(2)}) async-start(bf16[8,16,128]{2,1,0:T(8,128)(2,1)} %bitcast.6), calls=%async_computation.1 | async-start | bytes 65536 | tf_op jit(solution)/shard_map/all_to_all | solution.py:147
  49.9 5.2 %all-to-all-done.1 = bf16[8,16,128]{2,1,0:T(8,128)(2,1)S(1)} async-done(((bf16[8,16,128]{2,1,0:T(8,128)(2,1)}), bf16[8,16,128]{2,1,0:T(8,128)(2,1)S(1)}, u32[]{:S(2)}, u32[]{:S(2)}) %all-to-all-start.1) | async-done | bytes 32800 | tf_op jit(solution)/shard_map/all_to_all | solution.py:147
  56.4 8.5 %all-gather = f32[4,1,128]{2,1,0:T(1,128)} all-gather(f32[1,1,128]{2,1,0:T(1,128)S(1)} %bitcast.47), channel_id=1, replica_groups=mesh['blk'=4,'dp'=8] {'blk'}, dimensions={0}, use_global_device_ids=true | all-gather | bytes 2560 | tf_op jit(solution)/shard_map/all_gather | solution.py:153
  65.1 1.2 gather_fusion.3
  66.3 3.5 %all-to-all-start.2 = ((f32[8,16,128]{2,1,0:T(8,128)}), f32[8,16,128]{2,1,0:T(8,128)S(1)}, u32[]{:S(2)}, u32[]{:S(2)}) async-start(f32[8,16,128]{2,1,0:T(8,128)} %bitcast.11), calls=%async_computation.2 | async-start | bytes 131072 | tf_op jit(solution)/shard_map/all_to_all | solution.py:160
  69.9 1.2 fusion.13
  71.0 2.0 fusion.12
  73.1 0.9 copy.45
  74.0 1.7 all-to-all-done.2
  75.7 1.5 scatter_fusion
  77.3 1.8 fusion.44
  79.1 1.2 fusion.9
  80.3 0.9 fusion.40
  81.2 2.8 %fusion.36 = f32[2048,512]{1,0:T(8,128)} fusion(bf16[128,512]{1,0:T(8,128)(2,1)S(1)} %fusion.9, f32[128,2048]{1,0:T(8,128)S(1)} %copy.38, f32[128]{0:T(128)S(1)} %add_rsqrt_fusion, f32[128]{0:T(128)S(1)} %broadcast_multiply_fusion.4), kind=kOutput, calls=%fused_computation.91 | convolution fusion | flops 269221888 | bytes 5374976 | tf_op jit(solution)/shard_map/dot_general | solution.py:81
  84.1 1.4 subtract_multiply_fusion
  85.5 1.5 copy.48
  87.0 2.0 multiply_convert_fusion.1
  89.1 1.7 copy.49
  90.8 3.3 %convolution_bitcast_fusion = f32[256,128]{1,0:T(8,128)} fusion(bf16[128,32,256]{2,1,0:T(8,128)(2,1)} %copy-done.3, bf16[128,32,128]{2,1,0:T(8,128)(2,1)} %copy.49), kind=kOutput, calls=%fused_computation.19 | convolution fusion | flops 268435456 | bytes 3276800 | tf_op jit(solution)/shard_map/dot_general | solution.py:111
  95.3 143.1 %all-reduce.3.cloned.1.call-done = (f32[256,128]{1,0:T(8,128)}, f32[2048,512]{1,0:T(8,128)}, f32[512,128]{1,0:T(8,128)}) async-done(((f32[256,128]{1,0:T(8,128)}, f32[2048,512]{1,0:T(8,128)}, f32[512,128]{1,0:T(8,128)}), (f32[256,128]{1,0:T(8,128)}, f32[2048,512]{1,0:T(8,128)}, f32[512,128]{1,0:T(8,128)})) %all-reduce.3.cloned.1.call-update) | async-done | bytes 4587536 | tf_op jit(solution)/shard_map/psum | solution.py:173
  238.4 1.6 copy.60
  239.9 4.7 %copy.61 = f32[2048,512]{1,0:T(8,128)} copy(f32[2048,512]{1,0:T(8,128)} %get-tuple-element.33) | data formatting | bytes 8388608
  (71 shorter events, 9.3 us)
Async XLA Ops:
  7.2 23.3 %copy-start = (bf16[2048,512]{1,0:T(8,128)(2,1)S(1)}, bf16[2048,512]{1,0:T(8,128)(2,1)}, u32[]{:S(2)}) copy-start(bf16[2048,512]{1,0:T(8,128)(2,1)} %param.8) | copy-start | bytes 6291460
  12.8 28.7 %all-to-all-start = ((s32[8,1,16]{2,1,0:T(1,128)}), s32[8,1,16]{2,1,0:T(1,128)S(1)}, u32[]{:S(2)}, u32[]{:S(2)}) async-start(s32[8,1,16]{2,1,0:T(1,128)} %bitcast.4), calls=%async_computation | async-start | bytes 8192 | tf_op jit(solution)/shard_map/all_to_all | solution.py:145
  19.2 21.2 %copy-start.14 = (s32[128]{0:T(128)}, s32[128]{0:T(128)S(1)}, u32[]{:S(2)}) copy-start(s32[128]{0:T(128)S(1)} %iota_add_fusion) | copy-start | bytes 1540
  21.8 2.9 %copy-start.8 = (bf16[256,128]{1,0:T(8,128)(2,1)S(1)}, bf16[256,128]{1,0:T(8,128)(2,1)}, u32[]{:S(2)}) copy-start(bf16[256,128]{1,0:T(8,128)(2,1)} %param.7) | copy-start | bytes 196612
  24.7 2.5 %copy-start.3 = (bf16[128,32,256]{2,1,0:T(8,128)(2,1)}, bf16[128,32,256]{2,1,0:T(8,128)(2,1)S(1)}, u32[]{:S(2)}) copy-start(bf16[128,32,256]{2,1,0:T(8,128)(2,1)S(1)} %convert_bitcast_fusion) | copy-start | bytes 6291460
  27.3 1.3 copy-start.1
  27.8 1.2 copy-start.2
  30.5 1.2 copy-start.5
  31.7 9.7 %copy-start.6 = (bf16[128,512]{1,0:T(8,128)(2,1)}, bf16[128,512]{1,0:T(8,128)(2,1)S(1)}, u32[]{:S(2)}) copy-start(bf16[128,512]{1,0:T(8,128)(2,1)S(1)} %get-tuple-element.20) | copy-start | bytes 393220
  40.5 0.9 copy-start.7
  44.2 10.8 %all-to-all-start.1 = ((bf16[8,16,128]{2,1,0:T(8,128)(2,1)}), bf16[8,16,128]{2,1,0:T(8,128)(2,1)S(1)}, u32[]{:S(2)}, u32[]{:S(2)}) async-start(bf16[8,16,128]{2,1,0:T(8,128)(2,1)} %bitcast.6), calls=%async_computation.1 | async-start | bytes 65536 | tf_op jit(solution)/shard_map/all_to_all | solution.py:147
  55.9 9.1 %copy-start.9 = (f32[128]{0:T(128)}, f32[128]{0:T(128)S(1)}, u32[]{:S(2)}) copy-start(f32[128]{0:T(128)S(1)} %fusion.21) | copy-start | bytes 1540
  56.4 8.6 %copy-start.11 = (f32[128]{0:T(128)}, f32[128]{0:T(128)S(1)}, u32[]{:S(2)}) copy-start(f32[128]{0:T(128)S(1)} %get-tuple-element.15) | copy-start | bytes 1540
  66.3 9.3 %copy-start.13 = (s32[128]{0:T(128)S(1)}, s32[128]{0:T(128)}, u32[]{:S(2)}) copy-start(s32[128]{0:T(128)} %fusion.31) | copy-start | bytes 1540
  66.3 9.3 %all-to-all-start.2 = ((f32[8,16,128]{2,1,0:T(8,128)}), f32[8,16,128]{2,1,0:T(8,128)S(1)}, u32[]{:S(2)}, u32[]{:S(2)}) async-start(f32[8,16,128]{2,1,0:T(8,128)} %bitcast.11), calls=%async_computation.2 | async-start | bytes 131072 | tf_op jit(solution)/shard_map/all_to_all | solution.py:160
  69.8 168.5 %all-reduce.3.cloned.1.call-start = ((), (), s32[]{:S(2)}) async-start(), calls=%async_computation.3 | async-start | bytes 9175040 | tf_op jit(solution)/shard_map/psum | solution.py:173
  94.1 0.7 copy-start.10
  94.1 0.7 copy-start.12
  239.9 4.7 %copy-start.4 = (f32[512,128]{1,0:T(8,128)S(1)}, f32[512,128]{1,0:T(8,128)}, u32[]{:S(2)}) copy-start(f32[512,128]{1,0:T(8,128)} %get-tuple-element.34) | copy-start | bytes 786436
Sparse Core Ops, SparseCore 0:
  94.2 144.0 all-reduce.2
where the time goes:
time: 253 us; the launch traced here: 252 us
  waiting for transfers between devices  150 us (59%)
  matrix products  21 us (8%)
  local copies, waits for them, and re-layouts  20.8 us (8%)
  blocking collectives  17 us (7%)
  starting transfers between devices  15 us (6%)
  between operations  14.3 us (6%)
  other arithmetic  14.1 us (6%)
    psum x1, waiting for transfers between devices, on_device(): g_mix, g_in, g_out = lax.psum((g_mix, g_in, g_out), ('blk', 'dp'))  143 us
    all_gather x1, blocking collectives, on_device(): all_totals = lax.all_gather(totals, 'blk', axis=0, tiled=True)  8.55 us
    unnamed x33, local copies, waits for them, and re-layouts  8.52 us
    all_gather x1, blocking collectives, on_device(): lax.all_gather(units, 'blk', axis=0, tiled=True)  8.46 us
    all_to_all x1, starting transfers between devices, on_device(): lax.all_to_all(wanted, 'dp', split_axis=0, concat_axis=0, tiled=True)  6.35 us
    all_to_all x1, waiting for transfers between devices, on_device(): lax.all_to_all(picked, 'dp', split_axis=0, concat_axis=0, tiled=True)  5.16 us
    all_to_all x1, starting transfers between devices, on_device(): lax.all_to_all(picked, 'dp', split_axis=0, concat_axis=0, tiled=True)  5.09 us
  transfers between devices with their start and end apart: 4, of which 3 were waited for; matrix products, arithmetic and copies ran while one was open for 7% of the time, Pallas kernels for 0%

commit v1 on v0

--- a/solution.py
+++ b/solution.py
@@ -3,6 +3,7 @@
 import jax.numpy as jnp
 from jax import lax
 from jax.sharding import PartitionSpec as P
+from jax.lax import psum
 
 SCALE = 10.0
 
@@ -134,6 +135,10 @@
 
 
 def on_device(patches, w_mix, w_in, w_out, partner_dev, partner_row):
+
+    def map_tiles(patch):
+        return psum(psum(patch, "blk"), "dp")
+
     count = patches.shape[0]
     embed = w_out.shape[1]
     units, saved = encode(patches, w_mix, w_in, w_out)
@@ -170,7 +175,7 @@
     )
     g_in, g_out, norm_gradient = back_upper(grad_units, saved, w_in, w_out)
     g_mix = back_lower(norm_gradient, saved)
-    g_mix, g_in, g_out = lax.psum((g_mix, g_in, g_out), ("blk", "dp"))
+    g_mix, g_in, g_out = map_tiles((g_mix, g_in, g_out))
     return (loss_rows, g_mix, g_in, g_out)
 
 

time: 253 us -> 324 us (1.28)
  waiting for transfers between devices: 150 us -> 221 us
    psum x1 -> x2, waiting for transfers between devices: 143 us -> 214 us  [map_tiles(): return psum(psum(patch, 'blk'), 'dp')]
  transfers between devices with their start and end apart: 4 -> 5, of which waited for: 3 -> 4; matrix products, arithmetic and copies ran while one was open for 7% -> 6% of each run, Pallas kernels for 0% -> 0%
where the time goes in v1:
time: 324 us
  waiting for transfers between devices  221 us (68%)
  matrix products  21 us (6%)
  local copies, waits for them, and re-layouts  20.8 us (6%)
  blocking collectives  17 us (5%)
  starting transfers between devices  15 us (5%)
  between operations  14.3 us (4%)
  other arithmetic  14.1 us (4%)
    psum x2, waiting for transfers between devices, map_tiles(): return psum(psum(patch, 'blk'), 'dp')  214 us
    all_gather x1, blocking collectives, on_device(): all_totals = lax.all_gather(totals, 'blk', axis=0, tiled=True)  8.54 us
    unnamed x33, local copies, waits for them, and re-layouts  8.49 us
    all_gather x1, blocking collectives, on_device(): lax.all_gather(units, 'blk', axis=0, tiled=True)  8.46 us
  transfers between devices with their start and end apart: 5, of which 4 were waited for; matrix products, arithmetic and copies ran while one was open for 6% of the time, Pallas kernels for 0%

profile of v1, /device:TPU:0, one launch (start us, length us, event | category | flops | bytes accessed | tf_op | source)
XLA Modules:
  0.0 323.5 jit_solution(4429578687611284516)
XLA Ops:
  7.2 3.3 %sort.31 = (s32[128]{0:T(128)}, s32[128]{0:T(128)S(1)}) sort(s32[128]{0:T(128)} %param.10, s32[128]{0:T(128)S(1)} %iota.30), dimensions={0}, to_apply=%region_3.4 | sort | flops 896 | bytes 2048 | tf_op jit(solution)/shard_map/jit(argsort)/sort | solution.py:147
  10.5 1.6 gather_fusion
  12.8 6.4 %all-to-all-start = ((s32[8,1,16]{2,1,0:T(1,128)}), s32[8,1,16]{2,1,0:T(1,128)S(1)}, u32[]{:S(2)}, u32[]{:S(2)}) async-start(s32[8,1,16]{2,1,0:T(1,128)} %bitcast.4), calls=%async_computation | async-start | bytes 8192 | tf_op jit(solution)/shard_map/all_to_all | solution.py:150
  19.3 2.5 sort.32
  21.8 2.9 convert_bitcast_fusion
  24.8 2.5 fusion
  28.9 1.6 copy.38
  30.5 1.2 multiply_convert_fusion.2
  32.0 8.5 %all_gather.7 = bf16[512,128]{0,1:T(8,128)(2,1)S(1)} all-gather(bf16[128,128]{0,1:T(8,128)(2,1)S(1)} %fusion.35), channel_id=1, replica_groups=mesh['blk'=4,'dp'=8] {'blk'}, dimensions={0}, use_global_device_ids=true | all-gather | bytes 163840 | tf_op jit(solution)/shard_map/all_gather | solution.py:156
  42.9 1.3 gather_fusion.1
  44.2 5.1 %all-to-all-start.1 = ((bf16[8,16,128]{2,1,0:T(8,128)(2,1)}), bf16[8,16,128]{2,1,0:T(8,128)(2,1)S(1)}, u32[]{:S(2)}, u32[]{:S(2)}) async-start(bf16[8,16,128]{2,1,0:T(8,128)(2,1)} %bitcast.6), calls=%async_computation.1 | async-start | bytes 65536 | tf_op jit(solution)/shard_map/all_to_all | solution.py:152
  49.9 5.2 %all-to-all-done.1 = bf16[8,16,128]{2,1,0:T(8,128)(2,1)S(1)} async-done(((bf16[8,16,128]{2,1,0:T(8,128)(2,1)}), bf16[8,16,128]{2,1,0:T(8,128)(2,1)S(1)}, u32[]{:S(2)}, u32[]{:S(2)}) %all-to-all-start.1) | async-done | bytes 32800 | tf_op jit(solution)/shard_map/all_to_all | solution.py:152
  56.4 8.5 %all-gather = f32[4,1,128]{2,1,0:T(1,128)} all-gather(f32[1,1,128]{2,1,0:T(1,128)S(1)} %bitcast.47), channel_id=1, replica_groups=mesh['blk'=4,'dp'=8] {'blk'}, dimensions={0}, use_global_device_ids=true | all-gather | bytes 2560 | tf_op jit(solution)/shard_map/all_gather | solution.py:158
  65.1 1.2 gather_fusion.3
  66.3 3.5 %all-to-all-start.2 = ((f32[8,16,128]{2,1,0:T(8,128)}), f32[8,16,128]{2,1,0:T(8,128)S(1)}, u32[]{:S(2)}, u32[]{:S(2)}) async-start(f32[8,16,128]{2,1,0:T(8,128)} %bitcast.11), calls=%async_computation.2 | async-start | bytes 131072 | tf_op jit(solution)/shard_map/all_to_all | solution.py:165
  69.9 1.2 fusion.13
  71.0 2.0 fusion.12
  73.1 0.9 copy.45
  74.0 1.7 all-to-all-done.2
  75.7 1.5 scatter_fusion
  77.3 1.8 fusion.44
  79.1 1.2 fusion.9
  81.2 2.8 fusion.36
  84.1 1.4 subtract_multiply_fusion
  85.5 1.5 copy.48
  87.1 2.0 multiply_convert_fusion.1
  89.1 1.7 copy.49
  90.8 3.3 %convolution_bitcast_fusion = f32[256,128]{1,0:T(8,128)} fusion(bf16[128,32,256]{2,1,0:T(8,128)(2,1)} %copy-done.3, bf16[128,32,128]{2,1,0:T(8,128)(2,1)} %copy.49), kind=kOutput, calls=%fused_computation.19 | convolution fusion | flops 268435456 | bytes 3276800 | tf_op jit(solution)/shard_map/dot_general | solution.py:112
  94.2 109.0 %all-reduce.7.cloned.1.call-done = (f32[256,128]{1,0:T(8,128)}, f32[2048,512]{1,0:T(8,128)}, f32[512,128]{1,0:T(8,128)}) async-done(((f32[256,128]{1,0:T(8,128)}, f32[2048,512]{1,0:T(8,128)}, f32[512,128]{1,0:T(8,128)}), (f32[256,128]{1,0:T(8,128)}, f32[2048,512]{1,0:T(8,128)}, f32[512,128]{1,0:T(8,128)})) %all-reduce.7.cloned.1.call-update) | async-done | bytes 4587536 | tf_op jit(solution)/shard_map/psum | solution.py:140
  204.3 105.4 %all-reduce.5.cloned.1.call-done = (f32[256,128]{1,0:T(8,128)}, f32[2048,512]{1,0:T(8,128)}, f32[512,128]{1,0:T(8,128)}) async-done(((f32[256,128]{1,0:T(8,128)}, f32[2048,512]{1,0:T(8,128)}, f32[512,128]{1,0:T(8,128)}), (f32[256,128]{1,0:T(8,128)}, f32[2048,512]{1,0:T(8,128)}, f32[512,128]{1,0:T(8,128)})) %all-reduce.5.cloned.1.call-update) | async-done | bytes 4587536 | tf_op jit(solution)/shard_map/psum | solution.py:140
  309.7 1.6 copy.63
  311.3 4.7 %copy.64 = f32[2048,512]{1,0:T(8,128)} copy(f32[2048,512]{1,0:T(8,128)} %get-tuple-element.36) | data formatting | bytes 8388608
  (74 shorter events, 10.3 us)
Async XLA Ops:
  7.2 23.3 %copy-start = (bf16[2048,512]{1,0:T(8,128)(2,1)S(1)}, bf16[2048,512]{1,0:T(8,128)(2,1)}, u32[]{:S(2)}) copy-start(bf16[2048,512]{1,0:T(8,128)(2,1)} %param.8) | copy-start | bytes 6291460
  12.8 28.7 %all-to-all-start = ((s32[8,1,16]{2,1,0:T(1,128)}), s32[8,1,16]{2,1,0:T(1,128)S(1)}, u32[]{:S(2)}, u32[]{:S(2)}) async-start(s32[8,1,16]{2,1,0:T(1,128)} %bitcast.4), calls=%async_computation | async-start | bytes 8192 | tf_op jit(solution)/shard_map/all_to_all | solution.py:150
  19.2 21.2 %copy-start.14 = (s32[128]{0:T(128)}, s32[128]{0:T(128)S(1)}, u32[]{:S(2)}) copy-start(s32[128]{0:T(128)S(1)} %iota_add_fusion) | copy-start | bytes 1540
  21.8 2.9 copy-start.8
  24.7 2.5 copy-start.3
  27.3 1.3 copy-start.1
  27.8 1.2 copy-start.2
  30.5 1.2 copy-start.5
  31.7 9.7 %copy-start.6 = (bf16[128,512]{1,0:T(8,128)(2,1)}, bf16[128,512]{1,0:T(8,128)(2,1)S(1)}, u32[]{:S(2)}) copy-start(bf16[128,512]{1,0:T(8,128)(2,1)S(1)} %get-tuple-element.23) | copy-start | bytes 393220
  40.5 0.9 copy-start.7
  44.2 10.8 %all-to-all-start.1 = ((bf16[8,16,128]{2,1,0:T(8,128)(2,1)}), bf16[8,16,128]{2,1,0:T(8,128)(2,1)S(1)}, u32[]{:S(2)}, u32[]{:S(2)}) async-start(bf16[8,16,128]{2,1,0:T(8,128)(2,1)} %bitcast.6), calls=%async_computation.1 | async-start | bytes 65536 | tf_op jit(solution)/shard_map/all_to_all | solution.py:152
  55.9 9.1 %copy-start.9 = (f32[128]{0:T(128)}, f32[128]{0:T(128)S(1)}, u32[]{:S(2)}) copy-start(f32[128]{0:T(128)S(1)} %fusion.21) | copy-start | bytes 1540
  56.4 8.6 %copy-start.11 = (f32[128]{0:T(128)}, f32[128]{0:T(128)S(1)}, u32[]{:S(2)}) copy-start(f32[128]{0:T(128)S(1)} %get-tuple-element.18) | copy-start | bytes 1540
  66.3 9.3 %copy-start.13 = (s32[128]{0:T(128)S(1)}, s32[128]{0:T(128)}, u32[]{:S(2)}) copy-start(s32[128]{0:T(128)} %fusion.31) | copy-start | bytes 1540
  66.3 9.3 %all-to-all-start.2 = ((f32[8,16,128]{2,1,0:T(8,128)}), f32[8,16,128]{2,1,0:T(8,128)S(1)}, u32[]{:S(2)}, u32[]{:S(2)}) async-start(f32[8,16,128]{2,1,0:T(8,128)} %bitcast.11), calls=%async_computation.2 | async-start | bytes 131072 | tf_op jit(solution)/shard_map/all_to_all | solution.py:165
  69.8 133.3 %all-reduce.7.cloned.1.call-start = ((), (), s32[]{:S(2)}) async-start(), calls=%async_computation.4 | async-start | bytes 9175040 | tf_op jit(solution)/shard_map/psum | solution.py:140
  94.1 215.6 %all-reduce.5.cloned.1.call-start = ((), (), s32[]{:S(2)}) async-start(), calls=%async_computation.3 | async-start | bytes 9175040 | tf_op jit(solution)/shard_map/psum | solution.py:140
  203.1 0.6 copy-start.10
  203.1 0.6 copy-start.12
  311.3 4.7 %copy-start.4 = (f32[512,128]{1,0:T(8,128)S(1)}, f32[512,128]{1,0:T(8,128)}, u32[]{:S(2)}) copy-start(f32[512,128]{1,0:T(8,128)} %get-tuple-element.37) | copy-start | bytes 786436
Sparse Core Ops, SparseCore 0:
  94.3 108.8 all-reduce.6
  205.7 103.9 all-reduce.4
